TPU v7x, 32 devices: a whole 2x2x4 slice. The times are simulated.
32 devices in a mesh: row: 2 (over x), col: 16 (over z, y, core).
Axes of the slice: x: 2, y: 2, z: 4, core: 2. Of those that a mesh axis runs over, the one named last changes fastest.
Arguments:
- diagonal_tile: float32 [512, 512], P('row'), may hold values from -1 to 8, as said below
- panel: float32 [2048, 512], P(('row', 'col')), may hold values from -2.5 to 2.5
- trailing: bfloat16 [2048, 2048], P('col', 'row'), may hold values from -6 to 6
Outputs:
- factor_panel: float32 [2048, 512], P(('row', 'col'))
- updated: bfloat16 [2048, 2048], P('col', 'row')
Inputs may be any that keep to these rules, and one draw needn't show every extreme that they name: `diagonal_tile`: symmetric, and every eigenvalue is at least 1.
All inputs are finite; a program needn't handle non-finite values.
Results may differ from a plain program's by a relative error of at most 0.0085.
Values may be sent and summed in bfloat16 or wider, within the bound.
A program may use at most 64 MiB of HBM per device.

v0:
```python
import jax
import jax.numpy as jnp
from jax import lax
from jax.sharding import PartitionSpec as P


def per_device(diagonal_tile, panel, trailing):
    tile_whole = lax.all_gather(diagonal_tile, "row", axis=0, tiled=True)
    diag_factor = jnp.linalg.cholesky(tile_whole)

    def solve_rows(panel_rows):
        return jax.scipy.linalg.solve_triangular(diag_factor, panel_rows.T, lower=True).T

    factor_panel = solve_rows(panel)
    low_panel = factor_panel.astype(jnp.bfloat16)
    raw_rows = lax.all_gather(panel.astype(jnp.bfloat16), "row", axis=0, tiled=True).astype(
        panel.dtype
    )
    column_low = solve_rows(raw_rows).astype(jnp.bfloat16)
    block_low = lax.all_gather(low_panel, "col", axis=0, tiled=True)
    outer_term = lax.dot_general(
        column_low, block_low, (((1,), (1,)), ((), ())), preferred_element_type=jnp.float32
    )
    updated = (trailing.astype(jnp.float32) - outer_term).astype(jnp.bfloat16)
    return (factor_panel, updated)


def solution(mesh):
    return jax.shard_map(
        per_device,
        mesh=mesh,
        in_specs=(P("row", None), P(("row", "col"), None), P("col", "row")),
        out_specs=(P(("row", "col"), None), P("col", "row")),
        check_vma=False,
    )
```

profile of v0, /device:TPU:0, one launch (start us, length us, event | category | flops | bytes accessed | tf_op | source)
XLA Modules:
  0.0 216.5 jit_solution(180372973036767981)
XLA Ops:
  7.2 0.0 all-gather.3.cloned.1.call-start
  7.2 2.1 copy.5
  9.3 0.0 all-gather.3.cloned.1.call-update
  9.3 0.0 all-gather.5.cloned.1.call-start
  9.4 24.2 %all-gather.3.cloned.1.call-done = f32[512,512]{0,1:T(8,128)} async-done(((f32[256,512]{0,1:T(8,128)}), f32[512,512]{0,1:T(8,128)}) %all-gather.3.cloned.1.call-update) | async-done | bytes 1048592 | tf_op jit(solution)/shard_map/all_gather | solution.py:8
  33.6 0.0 copy-start
  33.6 1.6 copy.6
  35.2 0.0 copy-done
  35.2 0.2 fusion.1
  35.5 11.7 %cholesky.104 = f32[128,128]{1,0:T(8,128)S(1)} custom-call(f32[128,128]{1,0:T(8,128)S(1)} %cholesky.266), custom_call_target="Cholesky" | custom-call | tf_op jit(solution)/shard_map/jit(cholesky)/cholesky | solution.py:9
  47.2 9.8 %custom-call.34 = f32[1,128,128]{1,2,0:T(8,128)S(1)} custom-call(f32[1,128,128]{2,1,0:T(8,128)S(1)} %get-tuple-element.31), custom_call_target="InvertDiagBlocksLowerTriangular" | custom-call | tf_op jit(solution)/shard_map/jit(cholesky)/cholesky | solution.py:9
  57.0 0.1 cholesky.224
  57.2 0.3 constant_dynamic-update-slice_fusion.3
  57.5 0.3 convolution_subtract_fusion.1
  57.8 11.7 %cholesky.217 = f32[128,128]{1,0:T(8,128)S(1)} custom-call(f32[128,128]{1,0:T(8,128)S(1)} %cholesky.270), custom_call_target="Cholesky" | custom-call | tf_op jit(solution)/shard_map/jit(cholesky)/cholesky | solution.py:9
  69.6 10.0 %custom-call.35 = f32[1,128,128]{1,2,0:T(8,128)S(1)} custom-call(f32[1,128,128]{2,1,0:T(8,128)S(1)} %get-tuple-element.28), custom_call_target="InvertDiagBlocksLowerTriangular" | custom-call | tf_op jit(solution)/shard_map/jit(cholesky)/cholesky | solution.py:9
  79.5 0.3 convolution_dynamic-update-slice_fusion
  79.8 0.4 convolution_subtract_fusion.2
  80.2 11.7 %cholesky.238 = f32[128,128]{1,0:T(8,128)S(1)} custom-call(f32[128,128]{1,0:T(8,128)S(1)} %cholesky.275), custom_call_target="Cholesky" | custom-call | tf_op jit(solution)/shard_map/jit(cholesky)/cholesky | solution.py:9
  92.0 0.7 compare_reduce_fusion.1
  92.7 9.8 %custom-call.36 = f32[1,128,128]{1,2,0:T(8,128)S(1)} custom-call(f32[1,128,128]{2,1,0:T(8,128)S(1)} %get-tuple-element.25), custom_call_target="InvertDiagBlocksLowerTriangular" | custom-call | tf_op jit(solution)/shard_map/jit(cholesky)/cholesky | solution.py:9
  102.5 0.2 convolution_dynamic-update-slice_fusion.1
  102.7 0.4 convolution_subtract_fusion.6
  103.1 11.7 %cholesky.255 = f32[128,128]{1,0:T(8,128)S(1)} custom-call(f32[128,128]{1,0:T(8,128)S(1)} %convolution_subtract_fusion.6), custom_call_target="Cholesky" | custom-call | tf_op jit(solution)/shard_map/jit(cholesky)/cholesky | solution.py:9
  114.8 0.6 compare_reduce_fusion
  115.5 0.7 compare_reduce_fusion.2
  118.7 0.3 select_select_fusion
  119.0 0.0 copy-start.1
  119.0 8.5 %while.1 = (s32[]{:T(128)}, f32[512,512]{1,0:T(8,128)S(1)}, s32[4,2]{0,1:T(2,128)S(1)}, f32[4,128,128]{2,1,0:T(8,128)S(1)}, s32[]{:T(128)}) while((s32[]{:T(128)}, f32[512,512]{1,0:T(8,128)S(1)}, s32[4,2]{0,1:T(2,128)S(1)}, f32[4,128,128]{2,1,0:T(8,128)S(1)}, s32[]{:T(128)}) %tuple.35), condition=%wide.while_cond, body=%wide.while_body.sunk | while | flops 2 | bytes 131181 | solution.py:12
  119.1 0.1 constant_dynamic-slice_fusion.2
  119.1 0.6 fusion.72
  119.7 1.4 bitcast_dynamic-update-slice_fusion.2
  121.2 0.1 constant_dynamic-slice_fusion.2
  121.3 0.6 fusion.72
  121.9 1.4 bitcast_dynamic-update-slice_fusion.2
  123.3 0.1 constant_dynamic-slice_fusion.2
  123.4 0.6 fusion.72
  124.0 1.4 bitcast_dynamic-update-slice_fusion.2
  125.4 0.1 constant_dynamic-slice_fusion.2
  125.5 0.6 fusion.72
  126.1 1.4 bitcast_dynamic-update-slice_fusion.2
  127.5 39.3 %custom-call.37 = f32[4,128,128]{1,2,0:T(8,128)S(1)} custom-call(f32[4,128,128]{2,1,0:T(8,128)S(1)} %get-tuple-element.9), custom_call_target="InvertDiagBlocksLowerTriangular" | custom-call | tf_op jit(solution)/shard_map/jit(_solve_triangular)/triangular_solve | solution.py:12
  166.9 0.0 copy-done.1
  166.9 0.2 fusion.41
  167.1 0.2 convolution_subtract_fusion.9
  167.3 0.2 fusion.43
  167.5 0.3 convolution_subtract_fusion.8
  167.8 0.2 fusion.45
  168.0 0.4 convolution_subtract_fusion.7
  168.4 0.2 fusion.46
  168.6 0.7 fusion.56
  169.2 0.0 all-gather.5.cloned.1.call-update
  169.3 4.9 %all_gather.10 = bf16[128,512]{1,0:T(8,128)(2,1)S(1)} all-gather(bf16[64,512]{1,0:T(8,128)(2,1)S(1)} %convert_element_type.16), channel_id=1, replica_groups=mesh['row'=2,'col'=16] {'row'}, dimensions={0}, use_global_device_ids=true | all-gather | bytes 196608 | tf_op jit(solution)/shard_map/all_gather | solution.py:16
  174.2 0.3 fusion.60
  174.5 0.3 convolution_subtract_fusion.4
  174.8 0.3 fusion.59
  175.1 0.4 convolution_subtract_fusion.3
  175.5 0.3 fusion.58
  175.8 0.0 copy-start.2
  175.8 0.5 convolution_subtract_fusion.5
  176.3 0.3 convolution_convert_fusion
  176.6 30.7 %all-gather.5.cloned.1.call-done = bf16[1024,512]{1,0:T(8,128)(2,1)} async-done(((bf16[64,512]{1,0:T(8,128)(2,1)}), bf16[1024,512]{1,0:T(8,128)(2,1)}) %all-gather.5.cloned.1.call-update) | async-done | bytes 1048592 | tf_op jit(solution)/shard_map/all_gather | solution.py:20
  207.3 0.0 copy-done.2
  207.3 2.4 %fusion = bf16[128,1024]{1,0:T(8,128)(2,1)} fusion(bf16[1024,512]{1,0:T(8,128)(2,1)} %all-gather.5.cloned.1.call-done, bf16[128,1024]{1,0:T(8,128)(2,1)S(1)} %copy-done.2, bf16[128,128]{1,0:T(8,128)(2,1)S(1)} %convolution_convert_fusion, bf16[128,128]{1,0:T(8,128)(2,1)S(1)} %get-tuple-element.34, bf16[128,128]{1,0:T(8,128)(2,1)S(1)} %get-tuple-element.36, ...), kind=kOutput, calls=%fused_computation.3 | convolution fusion | flops 135135232 | bytes 1703936 | tf_op jit(solution)/shard_map/dot_general | solution.py:21
  (12 shorter events, 0.2 us)
Async XLA Ops:
  7.2 26.4 %all-gather.3.cloned.1.call-start = ((), (), s32[]{:S(2)}) async-start(), calls=%async_computation | async-start | bytes 1572864 | tf_op jit(solution)/shard_map/all_gather | solution.py:8
  9.3 198.0 %all-gather.5.cloned.1.call-start = ((), (), s32[]{:S(2)}) async-start(), calls=%async_computation.1 | async-start | bytes 1114112 | tf_op jit(solution)/shard_map/all_gather | solution.py:20
  33.6 1.7 copy-start
  119.0 47.8 %copy-start.1 = (f32[64,512]{1,0:T(8,128)S(1)}, f32[64,512]{1,0:T(8,128)}, u32[]{:S(2)}) copy-start(f32[64,512]{1,0:T(8,128)} %param.4) | copy-start | bytes 393220
  175.8 31.5 %copy-start.2 = (bf16[128,1024]{1,0:T(8,128)(2,1)S(1)}, bf16[128,1024]{1,0:T(8,128)(2,1)}, u32[]{:S(2)}) copy-start(bf16[128,1024]{1,0:T(8,128)(2,1)} %param.5) | copy-start | bytes 786436
Sparse Core Ops, SparseCore 0:
  9.5 23.9 all-gather.2
  169.4 37.8 all-gather.4
where the time goes:
time: 217 us
  other arithmetic  119 us (55%)
  waiting for transfers between devices  54.9 us (25%)
  between operations  16.9 us (8%)
  local copies, waits for them, and re-layouts  12.3 us (6%)
  matrix products  8.2 us (4%)
  blocking collectives  4.93 us (2%)
    another operation x14, other arithmetic, per_device(): diag_factor = jnp.linalg.cholesky(tile_whole)  78.6 us
    another operation x3, other arithmetic, solve_rows(): jax.scipy.linalg.solve_triangular(diag_factor, panel_rows.T, lower=True)  39.7 us
    all_gather x1, waiting for transfers between devices, per_device(): block_low = lax.all_gather(low_panel, 'col', axis=0, tiled=True)  30.7 us
    all_gather x1, waiting for transfers between devices, per_device(): tile_whole = lax.all_gather(diagonal_tile, 'row', axis=0, tiled=True)  24.2 us
    another operation x12, local copies, waits for them, and re-layouts  8.39 us
    all_gather x1, blocking collectives, per_device(): lax.all_gather(panel.astype(jnp.bfloat16), 'row', axis=0, tiled=True)  4.93 us
  transfers between devices with their start and end apart: 2, of which 2 were waited for; matrix products, arithmetic and copies ran while one was open for 1% of the time, Pallas kernels for 0%

commit v1 on v0

--- a/solution.py
+++ b/solution.py
@@ -17,7 +17,9 @@
         panel.dtype
     )
     column_low = solve_rows(raw_rows).astype(jnp.bfloat16)
-    block_low = lax.all_gather(low_panel, "col", axis=0, tiled=True)
+    block_low = jnp.concatenate(
+        lax.all_to_all(jnp.stack([low_panel] * lax.axis_size("col")), "col", 0, 0), axis=0
+    )
     outer_term = lax.dot_general(
         column_low, block_low, (((1,), (1,)), ((), ())), preferred_element_type=jnp.float32
     )

time: 217 us -> 208 us (0.959)
  waiting for transfers between devices: 54.9 us -> 39.7 us
  starting transfers between devices: 0.08 us -> 5.66 us
    all_gather x1 -> x0, waiting for transfers between devices: 30.7 us -> none  [per_device(): block_low = lax.all_gather(low_panel, 'col', axis=0, tiled=True)]
    all_to_all x0 -> x1, waiting for transfers between devices: none -> 15.4 us  [per_device(): lax.all_to_all(jnp.stack([low_panel] * lax.axis_size('col')), 'col', 0, 0)]
    all_to_all x0 -> x1, starting transfers between devices: none -> 5.62 us  [per_device(): lax.all_to_all(jnp.stack([low_panel] * lax.axis_size('col')), 'col', 0, 0)]
    another operation x12 -> x13, local copies, waits for them, and re-layouts: 8.39 us -> 9.48 us
where the time goes in v1:
time: 208 us; the launch traced here: 207 us
  other arithmetic  119 us (57%)
  waiting for transfers between devices  39.7 us (19%)
  between operations  16.9 us (8%)
  local copies, waits for them, and re-layouts  13.3 us (6%)
  matrix products  6.98 us (3%)
  starting transfers between devices  5.66 us (3%)
  blocking collectives  5.07 us (2%)
    another operation x14, other arithmetic, per_device(): diag_factor = jnp.linalg.cholesky(tile_whole)  78.8 us
    another operation x3, other arithmetic, solve_rows(): jax.scipy.linalg.solve_triangular(diag_factor, panel_rows.T, lower=True)  39.4 us
    all_gather x1, waiting for transfers between devices, per_device(): tile_whole = lax.all_gather(diagonal_tile, 'row', axis=0, tiled=True)  24.2 us
    all_to_all x1, waiting for transfers between devices, per_device(): lax.all_to_all(jnp.stack([low_panel] * lax.axis_size('col')), 'col', 0, 0)  15.4 us
    another operation x12, local copies, waits for them, and re-layouts  8.39 us
    all_to_all x1, starting transfers between devices, per_device(): lax.all_to_all(jnp.stack([low_panel] * lax.axis_size('col')), 'col', 0, 0)  5.62 us
    all_gather x1, blocking collectives, per_device(): lax.all_gather(panel.astype(jnp.bfloat16), 'row', axis=0, tiled=True)  5.07 us
  transfers between devices with their start and end apart: 2, of which 2 were waited for; matrix products, arithmetic and copies ran while one was open for 1% of the time, Pallas kernels for 0%

profile of v1, /device:TPU:0, one launch (start us, length us, event | category | flops | bytes accessed | tf_op | source)
XLA Modules:
  0.0 206.8 jit_solution(14678621344720530931)
XLA Ops:
  7.2 0.0 all-gather.2.cloned.1.call-start
  7.2 2.1 copy.5
  9.3 0.0 all-gather.2.cloned.1.call-update
  9.3 24.2 %all-gather.2.cloned.1.call-done = f32[512,512]{0,1:T(8,128)} async-done(((f32[256,512]{0,1:T(8,128)}), f32[512,512]{0,1:T(8,128)}) %all-gather.2.cloned.1.call-update) | async-done | bytes 1048592 | tf_op jit(solution)/shard_map/all_gather | solution.py:8
  33.6 0.0 copy-start
  33.6 1.6 copy.6
  35.2 0.0 copy-done
  35.2 0.2 fusion.1
  35.5 11.7 %cholesky.104 = f32[128,128]{1,0:T(8,128)S(1)} custom-call(f32[128,128]{1,0:T(8,128)S(1)} %cholesky.266), custom_call_target="Cholesky" | custom-call | tf_op jit(solution)/shard_map/jit(cholesky)/cholesky | solution.py:9
  47.2 9.8 %custom-call.34 = f32[1,128,128]{1,2,0:T(8,128)S(1)} custom-call(f32[1,128,128]{2,1,0:T(8,128)S(1)} %get-tuple-element.31), custom_call_target="InvertDiagBlocksLowerTriangular" | custom-call | tf_op jit(solution)/shard_map/jit(cholesky)/cholesky | solution.py:9
  57.0 0.1 cholesky.224
  57.2 0.3 constant_dynamic-update-slice_fusion.3
  57.5 0.3 convolution_subtract_fusion.1
  57.8 11.7 %cholesky.217 = f32[128,128]{1,0:T(8,128)S(1)} custom-call(f32[128,128]{1,0:T(8,128)S(1)} %cholesky.270), custom_call_target="Cholesky" | custom-call | tf_op jit(solution)/shard_map/jit(cholesky)/cholesky | solution.py:9
  69.6 9.9 %custom-call.35 = f32[1,128,128]{1,2,0:T(8,128)S(1)} custom-call(f32[1,128,128]{2,1,0:T(8,128)S(1)} %get-tuple-element.28), custom_call_target="InvertDiagBlocksLowerTriangular" | custom-call | tf_op jit(solution)/shard_map/jit(cholesky)/cholesky | solution.py:9
  79.5 0.3 convolution_dynamic-update-slice_fusion
  79.8 0.4 convolution_subtract_fusion.2
  80.2 11.7 %cholesky.238 = f32[128,128]{1,0:T(8,128)S(1)} custom-call(f32[128,128]{1,0:T(8,128)S(1)} %cholesky.275), custom_call_target="Cholesky" | custom-call | tf_op jit(solution)/shard_map/jit(cholesky)/cholesky | solution.py:9
  91.9 0.7 compare_reduce_fusion.1
  92.7 9.8 %custom-call.36 = f32[1,128,128]{1,2,0:T(8,128)S(1)} custom-call(f32[1,128,128]{2,1,0:T(8,128)S(1)} %get-tuple-element.25), custom_call_target="InvertDiagBlocksLowerTriangular" | custom-call | tf_op jit(solution)/shard_map/jit(cholesky)/cholesky | solution.py:9
  102.5 0.2 convolution_dynamic-update-slice_fusion.1
  102.7 0.4 convolution_subtract_fusion.6
  103.1 11.7 %cholesky.255 = f32[128,128]{1,0:T(8,128)S(1)} custom-call(f32[128,128]{1,0:T(8,128)S(1)} %convolution_subtract_fusion.6), custom_call_target="Cholesky" | custom-call | tf_op jit(solution)/shard_map/jit(cholesky)/cholesky | solution.py:9
  114.8 0.8 compare_reduce_fusion
  115.7 0.7 compare_reduce_fusion.2
  118.9 0.1 select_select_fusion
  119.0 0.0 copy-start.1
  119.0 8.5 %while.1 = (s32[]{:T(128)}, f32[512,512]{1,0:T(8,128)S(1)}, s32[4,2]{0,1:T(2,128)S(1)}, f32[4,128,128]{2,1,0:T(8,128)S(1)}, s32[]{:T(128)}) while((s32[]{:T(128)}, f32[512,512]{1,0:T(8,128)S(1)}, s32[4,2]{0,1:T(2,128)S(1)}, f32[4,128,128]{2,1,0:T(8,128)S(1)}, s32[]{:T(128)}) %tuple.35), condition=%wide.while_cond, body=%wide.while_body.sunk | while | flops 2 | bytes 131181 | solution.py:12
  119.0 0.1 constant_dynamic-slice_fusion.2
  119.1 0.6 fusion.72
  119.7 1.4 bitcast_dynamic-update-slice_fusion.2
  121.2 0.1 constant_dynamic-slice_fusion.2
  121.2 0.6 fusion.72
  121.8 1.4 bitcast_dynamic-update-slice_fusion.2
  123.3 0.1 constant_dynamic-slice_fusion.2
  123.4 0.6 fusion.72
  123.9 1.4 bitcast_dynamic-update-slice_fusion.2
  125.4 0.1 constant_dynamic-slice_fusion.2
  125.5 0.6 fusion.72
  126.1 1.4 bitcast_dynamic-update-slice_fusion.2
  127.5 39.3 %custom-call.37 = f32[4,128,128]{1,2,0:T(8,128)S(1)} custom-call(f32[4,128,128]{2,1,0:T(8,128)S(1)} %get-tuple-element.9), custom_call_target="InvertDiagBlocksLowerTriangular" | custom-call | tf_op jit(solution)/shard_map/jit(_solve_triangular)/triangular_solve | solution.py:12
  166.8 0.0 copy-done.1
  166.8 0.2 fusion.41
  167.0 0.2 convolution_subtract_fusion.9
  167.3 0.2 fusion.43
  167.5 0.3 convolution_subtract_fusion.8
  167.7 0.2 fusion.45
  167.9 0.4 convolution_subtract_fusion.7
  168.3 0.2 fusion.46
  168.5 0.7 fusion.56
  169.2 1.1 stack.2
  170.3 5.6 %all-to-all-start = ((bf16[16,64,512]{2,1,0:T(8,128)(2,1)}), bf16[16,64,512]{2,1,0:T(8,128)(2,1)S(1)}, u32[]{:S(2)}, u32[]{:S(2)}) async-start(bf16[16,64,512]{2,1,0:T(8,128)(2,1)} %stack.2), calls=%async_computation | async-start | bytes 2097152 | tf_op jit(solution)/shard_map/all_to_all | solution.py:21
  175.9 5.1 %all_gather.7 = bf16[128,512]{1,0:T(8,128)(2,1)S(1)} all-gather(bf16[64,512]{1,0:T(8,128)(2,1)S(1)} %convert_element_type.16), channel_id=1, replica_groups=mesh['row'=2,'col'=16] {'row'}, dimensions={0}, use_global_device_ids=true | all-gather | bytes 196608 | tf_op jit(solution)/shard_map/all_gather | solution.py:16
  181.0 0.2 fusion.60
  181.3 0.3 convolution_subtract_fusion.4
  181.6 0.3 fusion.59
  181.9 0.4 convolution_subtract_fusion.3
  182.3 0.3 fusion.58
  182.6 0.0 copy-start.2
  182.6 0.5 convolution_subtract_fusion.5
  183.1 0.3 convolution_convert_fusion
  183.4 15.4 %all-to-all-done = bf16[16,64,512]{2,1,0:T(8,128)(2,1)S(1)} async-done(((bf16[16,64,512]{2,1,0:T(8,128)(2,1)}), bf16[16,64,512]{2,1,0:T(8,128)(2,1)S(1)}, u32[]{:S(2)}, u32[]{:S(2)}) %all-to-all-start) | async-done | bytes 1048608 | tf_op jit(solution)/shard_map/all_to_all | solution.py:21
  198.8 0.0 copy-done.2
  198.8 1.2 fusion
  (12 shorter events, 0.2 us)
Async XLA Ops:
  7.2 26.4 %all-gather.2.cloned.1.call-start = ((), (), s32[]{:S(2)}) async-start(), calls=%async_computation.1 | async-start | bytes 1572864 | tf_op jit(solution)/shard_map/all_gather | solution.py:8
  33.6 1.7 copy-start
  119.0 47.8 %copy-start.1 = (f32[64,512]{1,0:T(8,128)S(1)}, f32[64,512]{1,0:T(8,128)}, u32[]{:S(2)}) copy-start(f32[64,512]{1,0:T(8,128)} %param.4) | copy-start | bytes 393220
  170.3 28.5 %all-to-all-start = ((bf16[16,64,512]{2,1,0:T(8,128)(2,1)}), bf16[16,64,512]{2,1,0:T(8,128)(2,1)S(1)}, u32[]{:S(2)}, u32[]{:S(2)}) async-start(bf16[16,64,512]{2,1,0:T(8,128)(2,1)} %stack.2), calls=%async_computation | async-start | bytes 2097152 | tf_op jit(solution)/shard_map/all_to_all | solution.py:21
  182.6 16.2 %copy-start.2 = (bf16[128,1024]{1,0:T(8,128)(2,1)S(1)}, bf16[128,1024]{1,0:T(8,128)(2,1)}, u32[]{:S(2)}) copy-start(bf16[128,1024]{1,0:T(8,128)(2,1)} %param.5) | copy-start | bytes 786436
Sparse Core Ops, SparseCore 0:
  9.5 23.9 all-gather.1
